TPU v7x, 32 devices: a whole 2x2x4 slice. The times are simulated.
32 devices in a mesh: rows: 16 (over z, y, x), grp: 2 (over core).
Axes of the slice: x: 2, y: 2, z: 4, core: 2. Of those that a mesh axis runs over, the one named last changes fastest.
Arguments:
- start_basis: bfloat16 [16384, 64], P(('rows', 'grp')), may hold values from -6 to 6
- kernel_blocks: bfloat16 [2944, 256, 256], P(('rows', 'grp')), may hold values from -0.0390625 to 0.0390625
- block_row: int32 [2944], P(('rows', 'grp')), may hold values from 0 to 63, as said below
- block_col: int32 [2944], P(('rows', 'grp')), may hold values from 0 to 63, as said below
- block_count: int32 [32], P(('rows', 'grp')), may hold values from 1 to 92, as said below
Outputs:
- embedding: float32 [16384, 64], P(('rows', 'grp'))
- projected: float32 [64, 64], replicated
Inputs may be any that keep to these rules, and one draw needn't show every extreme that they name: block_count[d] is the number of live slots of device d, its first ones; device 0 has all 92 live and the last device has 3. `block_row`: each slot's row block is one of its own device's 2 row blocks. `block_col`: each slot's column block is at least its row block; among one device's live slots at most 3 have their column block on any one device, the last device's live slots all lie on itself, and device 0 has a live slot whose column block lies on the last device.
All inputs are finite; a program needn't handle non-finite values.
Results may differ from a plain program's by a relative error of at most 0.0034.
Values may be sent and summed in bfloat16 or wider, within the bound.
A program may use at most 128 MiB of HBM per device.

v0:
```python
import jax
import jax.numpy as jnp
from jax import lax
from jax.sharding import PartitionSpec as P

ITERS = 2


def onehot(index, count, dtype):
    return (index[:, None] == jnp.arange(count, dtype=jnp.int32)[None, :]).astype(dtype)


def on_device(start_basis, kernel_blocks, block_row, block_col, block_count):
    devices = lax.axis_size(("rows", "grp"))
    my_index = lax.axis_index(("rows", "grp"))
    block_size = kernel_blocks.shape[1]
    columns = start_basis.shape[1]
    own_rows = start_basis.shape[0]
    row_blocks = own_rows // block_size
    slot_count = kernel_blocks.shape[0]
    per_peer = (slot_count + devices - 1) // devices
    total_rows = own_rows * devices
    outside = devices * per_peer
    positions = jnp.arange(slot_count, dtype=jnp.int32)
    alive_mask = positions < block_count[0]
    local_row = block_row - my_index * row_blocks
    target = block_col // row_blocks
    target_block = block_col - target * row_blocks
    earlier = (
        (target[:, None] == target[None, :])
        & alive_mask[None, :]
        & (positions[None, :] < positions[:, None])
    )
    order_rank = jnp.sum(earlier.astype(jnp.int32), axis=1)
    slot_place = jnp.where(alive_mask, target * per_peer + order_rank, outside)
    wanted_local = jnp.full((outside,), -1, jnp.int32).at[slot_place].set(target_block, mode="drop")
    incoming = lax.all_to_all(
        wanted_local, ("rows", "grp"), split_axis=0, concat_axis=0, tiled=True
    )
    row_select = (
        onehot(local_row, row_blocks, jnp.float32) * alive_mask[:, None].astype(jnp.float32)
    ).T
    reply_select = onehot(incoming, row_blocks, jnp.bfloat16)
    receive_select = reply_select.T
    basis = start_basis
    result = None
    projected = None
    for iteration in range(ITERS):
        basis_tiles = basis.reshape(row_blocks, block_size, columns)
        gathered = lax.all_gather(basis, ("rows", "grp"), axis=0, tiled=True)
        partners = jnp.take(gathered.reshape(-1, block_size, columns), block_col, axis=0)
        forward = jnp.einsum(
            "sij,sjc->sic", kernel_blocks, partners, preferred_element_type=jnp.float32
        )
        own_tiles = jnp.take(basis_tiles, local_row, axis=0)
        mirrored = jnp.einsum(
            "sji,sjc->sic", kernel_blocks, own_tiles, preferred_element_type=jnp.float32
        ).astype(jnp.bfloat16)
        outgoing = (
            jnp.zeros((outside, block_size, columns), jnp.bfloat16)
            .at[slot_place]
            .set(mirrored, mode="drop")
        )
        arrived = lax.all_to_all(outgoing, ("rows", "grp"), split_axis=0, concat_axis=0, tiled=True)
        image_rows = jnp.einsum("ks,sic->kic", row_select, forward, precision=lax.Precision.HIGHEST)
        image_rows = image_rows + jnp.einsum(
            "kr,ric->kic", receive_select, arrived, preferred_element_type=jnp.float32
        )
        flat_image = image_rows.reshape(own_rows, columns)
        gram_part = jnp.dot(flat_image.T, flat_image, precision=lax.Precision.HIGHEST)
        if iteration == ITERS - 1:
            projection = jnp.dot(
                basis.astype(jnp.float32).T, flat_image, precision=lax.Precision.HIGHEST
            )
            gram_part, projection = lax.psum((gram_part, projection), ("rows", "grp"))
            projected = projection / total_rows
        else:
            gram_part = lax.psum(gram_part, ("rows", "grp"))
        lower_factor = jnp.linalg.cholesky(gram_part / total_rows)
        inverse = jax.scipy.linalg.solve_triangular(
            lower_factor, jnp.eye(columns, dtype=jnp.float32), lower=True
        )
        result = jnp.dot(flat_image, inverse.T, precision=lax.Precision.HIGHEST)
        basis = result.astype(jnp.bfloat16)
    return (result, projected)


def solution(mesh):
    in_specs = (
        P(("rows", "grp"), None),
        P(("rows", "grp"), None, None),
        P(("rows", "grp")),
        P(("rows", "grp")),
        P(("rows", "grp")),
    )
    out_specs = (P(("rows", "grp"), None), P())
    return jax.shard_map(
        on_device, mesh=mesh, in_specs=in_specs, out_specs=out_specs, check_vma=False
    )
```

profile of v0, /device:TPU:0, one launch (start us, length us, event | category | flops | bytes accessed | tf_op | source)
XLA Modules:
  0.0 407.3 jit_solution(14491948732641696692)
XLA Ops:
  10.3 7.3 %all-to-all-start = ((s32[32,3,1]{1,2,0:T(1,128)}), s32[32,3,1]{1,2,0:T(1,128)S(1)}, u32[]{:S(2)}, u32[]{:S(2)}) async-start(s32[32,3,1]{1,2,0:T(1,128)} %bitcast.3), calls=%async_computation | async-start | bytes 32768 | tf_op jit(solution)/shard_map/all_to_all | solution.py:37
  19.9 8.3 %convert_bitcast_fusion.1 = bf16[92,256,64]{1,2,0:T(8,128)(2,1)} fusion(bf16[92,256,256]{2,1,0:T(8,128)(2,1)} %param.13, bf16[92,256,64]{1,2,0:T(8,128)(2,1)S(1)} %gather_fusion.1, pred[92]{0:T(512)(128)(4,1)S(1)} %get-tuple-element.20), kind=kOutput, calls=%fused_computation.24 | convolution fusion | flops 774766592 | bytes 18088028 | tf_op jit(solution)/shard_map/sji,sjc->sic/dot_general | solution.py:56
  31.2 12.6 %scatter_fusion = bf16[96,256,64]{1,2,0:T(8,128)(2,1)} fusion(bf16[96,256,64]{1,2,0:T(8,128)(2,1)} %broadcast.76.clone, s32[92]{0:T(128)S(1)} %compare_select_fusion.1, bf16[92,256,64]{1,2,0:T(8,128)(2,1)S(1)} %copy-done.1), kind=kCustom, calls=%fused_computation.5 | custom fusion | bytes 9044336 | tf_op jit(solution)/shard_map/scatter | solution.py:62
  43.8 7.4 %all-to-all-start.1 = ((bf16[96,256,64]{1,2,0:T(8,128)(2,1)}), bf16[96,256,64]{1,2,0:T(8,128)(2,1)}, u32[]{:S(2)}, u32[]{:S(2)}) async-start(bf16[96,256,64]{1,2,0:T(8,128)(2,1)} %scatter_fusion), calls=%async_computation.1 | async-start | bytes 6291456 | tf_op jit(solution)/shard_map/all_to_all | solution.py:64
  53.3 72.3 %all-gather.3.cloned.1.call-done = bf16[16384,64]{0,1:T(8,128)(2,1)} async-done(((bf16[512,64]{0,1:T(8,128)(2,1)}), bf16[16384,64]{0,1:T(8,128)(2,1)}) %all-gather.3.cloned.1.call-update) | async-done | bytes 2097168 | tf_op jit(solution)/shard_map/all_gather | solution.py:50
  127.4 2.5 gather_fusion
  130.0 11.7 %fusion.20 = f32[92,256,64]{1,2,0:T(8,128)} fusion(bf16[92,256,256]{2,1,0:T(8,128)(2,1)} %param.13, bf16[92,256,64]{1,2,0:T(8,128)(2,1)} %gather_fusion, pred[92]{0:T(512)(128)(4,1)S(1)} %compare_and_fusion), kind=kOutput, calls=%fused_computation.29 | convolution fusion | flops 773259264 | bytes 21102684 | tf_op jit(solution)/shard_map/sij,sjc->sic/dot_general | solution.py:52
  141.6 9.3 %fusion.2 = f32[2,256,64]{1,0,2:T(2,128)S(1)} fusion(f32[92,256,64]{1,2,0:T(8,128)} %fusion.20, f32[92]{0:T(128)S(1)} %fusion.74, s32[92]{0:T(128)S(1)} %get-tuple-element.21), kind=kOutput, calls=%fused_computation.9 | convolution fusion | flops 36176240 | bytes 6161120 | tf_op jit(solution)/shard_map/ks,sic->kic/dot_general | solution.py:65
  151.0 3.7 fusion.34
  155.0 40.9 %psum.21 = f32[64,64]{0,1:T(8,128)S(1)} all-reduce(f32[64,64]{0,1:T(8,128)S(1)} %convolution_bitcast_fusion.1), channel_id=1, replica_groups=mesh['rows'=16,'grp'=2] {'rows','grp'}, use_global_device_ids=true, to_apply=%region_3.6 | all-reduce | flops 4096 | bytes 32768 | tf_op jit(solution)/shard_map/psum | solution.py:78
  196.0 5.8 %cholesky.44 = f32[64,64]{1,0:T(8,128)S(1)} custom-call(f32[64,64]{1,0:T(8,128)S(1)} %fusion.52), custom_call_target="Cholesky" | custom-call | tf_op jit(solution)/shard_map/jit(cholesky)/cholesky | solution.py:79
  203.2 4.9 %custom-call.6 = f32[1,64,64]{1,2,0:T(8,128)S(1)} custom-call(f32[1,64,64]{2,1,0:T(8,128)S(1)} %fusion.47), custom_call_target="InvertDiagBlocksLowerTriangular" | custom-call | tf_op jit(solution)/shard_map/jit(_solve_triangular)/triangular_solve | solution.py:80
  209.4 8.3 %convert_bitcast_fusion = bf16[92,256,64]{1,2,0:T(8,128)(2,1)} fusion(bf16[92,256,256]{2,1,0:T(8,128)(2,1)} %param.13, bf16[92,256,64]{1,2,0:T(8,128)(2,1)S(1)} %gather_fusion.3, pred[92]{0:T(512)(128)(4,1)S(1)} %get-tuple-element.20), kind=kOutput, calls=%fused_computation.23 | convolution fusion | flops 774766592 | bytes 18088028 | tf_op jit(solution)/shard_map/sji,sjc->sic/dot_general | solution.py:56
  217.7 2.0 broadcast.76
  220.7 12.6 %scatter_fusion.1 = bf16[96,256,64]{1,2,0:T(8,128)(2,1)} fusion(bf16[96,256,64]{1,2,0:T(8,128)(2,1)} %broadcast.76, s32[92]{0:T(128)S(1)} %compare_select_fusion.1, bf16[92,256,64]{1,2,0:T(8,128)(2,1)S(1)} %copy-done), kind=kCustom, calls=%fused_computation.6 | custom fusion | bytes 9044336 | tf_op jit(solution)/shard_map/scatter | solution.py:62
  233.3 5.4 %all-to-all-start.2 = ((bf16[96,256,64]{1,2,0:T(8,128)(2,1)}), bf16[96,256,64]{1,2,0:T(8,128)(2,1)}, u32[]{:S(2)}, u32[]{:S(2)}) async-start(bf16[96,256,64]{1,2,0:T(8,128)(2,1)} %scatter_fusion.1), calls=%async_computation.2 | async-start | bytes 6291456 | tf_op jit(solution)/shard_map/all_to_all | solution.py:64
  239.4 79.1 %all-gather.5.cloned.1.call-done = bf16[16384,64]{0,1:T(8,128)(2,1)} async-done(((bf16[512,64]{0,1:T(8,128)(2,1)}), bf16[16384,64]{0,1:T(8,128)(2,1)}) %all-gather.5.cloned.1.call-update) | async-done | bytes 2097168 | tf_op jit(solution)/shard_map/all_gather | solution.py:50
  320.4 2.5 gather_fusion.2
  323.0 11.7 %fusion.23 = f32[92,256,64]{1,2,0:T(8,128)} fusion(bf16[92,256,256]{2,1,0:T(8,128)(2,1)} %param.13, bf16[92,256,64]{1,2,0:T(8,128)(2,1)} %gather_fusion.2, pred[92]{0:T(512)(128)(4,1)S(1)} %compare_and_fusion), kind=kOutput, calls=%fused_computation.30 | convolution fusion | flops 773259264 | bytes 21102684 | tf_op jit(solution)/shard_map/sij,sjc->sic/dot_general | solution.py:52
  334.6 9.3 %fusion = f32[2,256,64]{1,0,2:T(2,128)S(1)} fusion(f32[92,256,64]{1,2,0:T(8,128)} %fusion.23, f32[92]{0:T(128)S(1)} %fusion.74, s32[92]{0:T(128)S(1)} %get-tuple-element.21), kind=kOutput, calls=%fused_computation.7 | convolution fusion | flops 36176240 | bytes 6161120 | tf_op jit(solution)/shard_map/ks,sic->kic/dot_general | solution.py:65
  344.0 3.7 fusion.37
  348.2 38.2 %all-reduce = (f32[64,64]{0,1:T(8,128)S(1)}, f32[64,64]{0,1:T(8,128)S(1)}) all-reduce(f32[64,64]{0,1:T(8,128)S(1)} %convolution_bitcast_fusion, f32[64,64]{0,1:T(8,128)S(1)} %fusion.76), channel_id=1, replica_groups=mesh['rows'=16,'grp'=2] {'rows','grp'}, use_global_device_ids=true, to_apply=%region_7.12 | all-reduce | flops 8192 | bytes 65536 | tf_op jit(solution)/shard_map/psum | solution.py:75
  386.5 5.8 %cholesky.55 = f32[64,64]{1,0:T(8,128)S(1)} custom-call(f32[64,64]{1,0:T(8,128)S(1)} %fusion.50), custom_call_target="Cholesky" | custom-call | tf_op jit(solution)/shard_map/jit(cholesky)/cholesky | solution.py:79
  393.7 4.9 %custom-call.7 = f32[1,64,64]{1,2,0:T(8,128)S(1)} custom-call(f32[1,64,64]{2,1,0:T(8,128)S(1)} %fusion.48), custom_call_target="InvertDiagBlocksLowerTriangular" | custom-call | tf_op jit(solution)/shard_map/jit(_solve_triangular)/triangular_solve | solution.py:80
  (61 shorter events, 22.0 us)
Async XLA Ops:
  10.3 33.5 %all-to-all-start = ((s32[32,3,1]{1,2,0:T(1,128)}), s32[32,3,1]{1,2,0:T(1,128)S(1)}, u32[]{:S(2)}, u32[]{:S(2)}) async-start(s32[32,3,1]{1,2,0:T(1,128)} %bitcast.3), calls=%async_computation | async-start | bytes 32768 | tf_op jit(solution)/shard_map/all_to_all | solution.py:37
  28.2 3.0 copy-start.1
  43.8 8.1 %copy-start.4 = (s32[92]{0:T(128)S(1)}, s32[92]{0:T(128)}, u32[]{:S(2)}) copy-start(s32[92]{0:T(128)} %param.15) | copy-start | bytes 1108
  43.8 107.2 %all-to-all-start.1 = ((bf16[96,256,64]{1,2,0:T(8,128)(2,1)}), bf16[96,256,64]{1,2,0:T(8,128)(2,1)}, u32[]{:S(2)}, u32[]{:S(2)}) async-start(bf16[96,256,64]{1,2,0:T(8,128)(2,1)} %scatter_fusion), calls=%async_computation.1 | async-start | bytes 6291456 | tf_op jit(solution)/shard_map/all_to_all | solution.py:64
  51.2 74.4 %all-gather.3.cloned.1.call-start = ((), (), s32[]{:S(2)}) async-start(), calls=%async_computation.3 | async-start | bytes 2162688 | tf_op jit(solution)/shard_map/all_gather | solution.py:50
  208.6 0.8 copy-start.2
  217.7 3.0 copy-start
  233.3 110.7 %all-to-all-start.2 = ((bf16[96,256,64]{1,2,0:T(8,128)(2,1)}), bf16[96,256,64]{1,2,0:T(8,128)(2,1)}, u32[]{:S(2)}, u32[]{:S(2)}) async-start(bf16[96,256,64]{1,2,0:T(8,128)(2,1)} %scatter_fusion.1), calls=%async_computation.2 | async-start | bytes 6291456 | tf_op jit(solution)/shard_map/all_to_all | solution.py:64
  238.7 79.8 %all-gather.5.cloned.1.call-start = ((), (), s32[]{:S(2)}) async-start(), calls=%async_computation.4 | async-start | bytes 2162688 | tf_op jit(solution)/shard_map/all_gather | solution.py:50
  344.0 4.0 copy-start.3
Sparse Core Ops, SparseCore 0:
  54.9 70.6 all-gather.2
  243.0 75.5 all-gather.4
where the time goes:
time: 410 us; the launch traced here: 407 us
  waiting for transfers between devices  152 us (37%)
  blocking collectives  79.1 us (19%)
  matrix products  68.4 us (17%)
  local copies, waits for them, and re-layouts  45.5 us (11%)
  other arithmetic  26.4 us (6%)
  starting transfers between devices  20.6 us (5%)
  between operations  15 us (4%)
    all_gather x2, waiting for transfers between devices, on_device(): gathered = lax.all_gather(basis, ('rows', 'grp'), axis=0, tiled=True)  151 us
    psum x1, blocking collectives, on_device(): gram_part = lax.psum(gram_part, ('rows', 'grp'))  40.9 us
    psum x1, blocking collectives, on_device(): gram_part, projection = lax.psum((gram_part, projection), ('rows', 'grp'))  38.2 us
    scatter x2, local copies, waits for them, and re-layouts, on_device(): outgoing = jnp.zeros((outside, block_size, columns), jnp.bfloat16).at[slo...  25.2 us
    dot_general x2, matrix products, on_device(): jnp.einsum('sij,sjc->sic', kernel_blocks, partners, preferred_element_typ...  23.3 us
    dot_general x2, matrix products, on_device(): jnp.einsum('ks,sic->kic', row_select, forward, precision=lax.Precision.HI...  18.7 us
    dot_general x2, matrix products, on_device(): jnp.einsum('sji,sjc->sic', kernel_blocks, own_tiles, preferred_element_ty...  16.6 us
    another operation x6, other arithmetic, on_device(): lower_factor = jnp.linalg.cholesky(gram_part / total_rows)  13 us
  transfers between devices with their start and end apart: 5, of which 2 were waited for; matrix products, arithmetic and copies ran while one was open for 19% of the time, Pallas kernels for 0%

commit v1 on v0

--- a/solution.py
+++ b/solution.py
@@ -75,7 +75,7 @@
             gram_part, projection = lax.psum((gram_part, projection), ("rows", "grp"))
             projected = projection / total_rows
         else:
-            gram_part = lax.psum(gram_part, ("rows", "grp"))
+            gram_part = lax.psum(lax.psum(gram_part, "grp"), "rows")
         lower_factor = jnp.linalg.cholesky(gram_part / total_rows)
         inverse = jax.scipy.linalg.solve_triangular(
             lower_factor, jnp.eye(columns, dtype=jnp.float32), lower=True

time: 410 us -> 446 us (1.088)
  blocking collectives: 79.1 us -> 119 us
    psum x1 -> x2, blocking collectives: 40.9 us -> 79.2 us  [on_device(): gram_part = lax.psum(lax.psum(gram_part, 'grp'), 'rows')]
  transfers between devices with their start and end apart: 5 -> 5, of which waited for: 2 -> 2; matrix products, arithmetic and copies ran while one was open for 19% -> 17% of each run, Pallas kernels for 0% -> 0%
where the time goes in v1:
time: 446 us; the launch traced here: 444 us
  waiting for transfers between devices  151 us (34%)
  blocking collectives  119 us (27%)
  matrix products  68.4 us (15%)
  local copies, waits for them, and re-layouts  45.5 us (10%)
  other arithmetic  26.4 us (6%)
  starting transfers between devices  18.5 us (4%)
  between operations  15 us (3%)
    all_gather x2, waiting for transfers between devices, on_device(): gathered = lax.all_gather(basis, ('rows', 'grp'), axis=0, tiled=True)  150 us
    psum x2, blocking collectives, on_device(): gram_part = lax.psum(lax.psum(gram_part, 'grp'), 'rows')  79.2 us
    psum x1, blocking collectives, on_device(): gram_part, projection = lax.psum((gram_part, projection), ('rows', 'grp'))  39.7 us
    scatter x2, local copies, waits for them, and re-layouts, on_device(): outgoing = jnp.zeros((outside, block_size, columns), jnp.bfloat16).at[slo...  25.2 us
    dot_general x2, matrix products, on_device(): jnp.einsum('sij,sjc->sic', kernel_blocks, partners, preferred_element_typ...  23.3 us
    dot_general x2, matrix products, on_device(): jnp.einsum('ks,sic->kic', row_select, forward, precision=lax.Precision.HI...  18.7 us
    dot_general x2, matrix products, on_device(): jnp.einsum('sji,sjc->sic', kernel_blocks, own_tiles, preferred_element_ty...  16.6 us
    another operation x6, other arithmetic, on_device(): lower_factor = jnp.linalg.cholesky(gram_part / total_rows)  13 us
  transfers between devices with their start and end apart: 5, of which 2 were waited for; matrix products, arithmetic and copies ran while one was open for 17% of the time, Pallas kernels for 0%

profile of v1, /device:TPU:0, one launch (start us, length us, event | category | flops | bytes accessed | tf_op | source)
XLA Modules:
  0.0 443.6 jit_solution(12535678995025768321)
XLA Ops:
  10.3 7.3 %all-to-all-start = ((s32[32,3,1]{1,2,0:T(1,128)}), s32[32,3,1]{1,2,0:T(1,128)S(1)}, u32[]{:S(2)}, u32[]{:S(2)}) async-start(s32[32,3,1]{1,2,0:T(1,128)} %bitcast.3), calls=%async_computation | async-start | bytes 32768 | tf_op jit(solution)/shard_map/all_to_all | solution.py:37
  19.9 8.3 %convert_bitcast_fusion.1 = bf16[92,256,64]{1,2,0:T(8,128)(2,1)} fusion(bf16[92,256,256]{2,1,0:T(8,128)(2,1)} %param.13, bf16[92,256,64]{1,2,0:T(8,128)(2,1)S(1)} %gather_fusion.1, pred[92]{0:T(512)(128)(4,1)S(1)} %get-tuple-element.20), kind=kOutput, calls=%fused_computation.24 | convolution fusion | flops 774766592 | bytes 18088028 | tf_op jit(solution)/shard_map/sji,sjc->sic/dot_general | solution.py:56
  31.2 12.6 %scatter_fusion = bf16[96,256,64]{1,2,0:T(8,128)(2,1)} fusion(bf16[96,256,64]{1,2,0:T(8,128)(2,1)} %broadcast.76.clone, s32[92]{0:T(128)S(1)} %compare_select_fusion.1, bf16[92,256,64]{1,2,0:T(8,128)(2,1)S(1)} %copy-done.1), kind=kCustom, calls=%fused_computation.5 | custom fusion | bytes 9044336 | tf_op jit(solution)/shard_map/scatter | solution.py:62
  43.8 7.4 %all-to-all-start.1 = ((bf16[96,256,64]{1,2,0:T(8,128)(2,1)}), bf16[96,256,64]{1,2,0:T(8,128)(2,1)}, u32[]{:S(2)}, u32[]{:S(2)}) async-start(bf16[96,256,64]{1,2,0:T(8,128)(2,1)} %scatter_fusion), calls=%async_computation.1 | async-start | bytes 6291456 | tf_op jit(solution)/shard_map/all_to_all | solution.py:64
  53.3 72.3 %all-gather.3.cloned.1.call-done = bf16[16384,64]{0,1:T(8,128)(2,1)} async-done(((bf16[512,64]{0,1:T(8,128)(2,1)}), bf16[16384,64]{0,1:T(8,128)(2,1)}) %all-gather.3.cloned.1.call-update) | async-done | bytes 2097168 | tf_op jit(solution)/shard_map/all_gather | solution.py:50
  127.4 2.5 gather_fusion
  130.0 11.7 %fusion.20 = f32[92,256,64]{1,2,0:T(8,128)} fusion(bf16[92,256,256]{2,1,0:T(8,128)(2,1)} %param.13, bf16[92,256,64]{1,2,0:T(8,128)(2,1)} %gather_fusion, pred[92]{0:T(512)(128)(4,1)S(1)} %compare_and_fusion), kind=kOutput, calls=%fused_computation.29 | convolution fusion | flops 773259264 | bytes 21102684 | tf_op jit(solution)/shard_map/sij,sjc->sic/dot_general | solution.py:52
  141.6 9.3 %fusion.2 = f32[2,256,64]{1,0,2:T(2,128)S(1)} fusion(f32[92,256,64]{1,2,0:T(8,128)} %fusion.20, f32[92]{0:T(128)S(1)} %fusion.74, s32[92]{0:T(128)S(1)} %get-tuple-element.21), kind=kOutput, calls=%fused_computation.9 | convolution fusion | flops 36176240 | bytes 6161120 | tf_op jit(solution)/shard_map/ks,sic->kic/dot_general | solution.py:65
  151.0 3.7 fusion.34
  155.0 3.5 psum.28
  158.5 75.7 %psum.29 = f32[64,64]{0,1:T(8,128)S(1)} all-reduce(f32[64,64]{0,1:T(8,128)S(1)} %psum.28), channel_id=1, replica_groups=mesh['rows'=16,'grp'=2] {'rows'}, use_global_device_ids=true, to_apply=%region_4.7 | all-reduce | flops 4096 | bytes 32768 | tf_op jit(solution)/shard_map/psum | solution.py:78
  234.2 5.8 %cholesky.44 = f32[64,64]{1,0:T(8,128)S(1)} custom-call(f32[64,64]{1,0:T(8,128)S(1)} %fusion.52), custom_call_target="Cholesky" | custom-call | tf_op jit(solution)/shard_map/jit(cholesky)/cholesky | solution.py:79
  241.4 4.9 %custom-call.6 = f32[1,64,64]{1,2,0:T(8,128)S(1)} custom-call(f32[1,64,64]{2,1,0:T(8,128)S(1)} %fusion.47), custom_call_target="InvertDiagBlocksLowerTriangular" | custom-call | tf_op jit(solution)/shard_map/jit(_solve_triangular)/triangular_solve | solution.py:80
  247.7 8.3 %convert_bitcast_fusion = bf16[92,256,64]{1,2,0:T(8,128)(2,1)} fusion(bf16[92,256,256]{2,1,0:T(8,128)(2,1)} %param.13, bf16[92,256,64]{1,2,0:T(8,128)(2,1)S(1)} %gather_fusion.3, pred[92]{0:T(512)(128)(4,1)S(1)} %get-tuple-element.20), kind=kOutput, calls=%fused_computation.23 | convolution fusion | flops 774766592 | bytes 18088028 | tf_op jit(solution)/shard_map/sji,sjc->sic/dot_general | solution.py:56
  258.9 12.6 %scatter_fusion.1 = bf16[96,256,64]{1,2,0:T(8,128)(2,1)} fusion(bf16[96,256,64]{1,2,0:T(8,128)(2,1)} %broadcast.76, s32[92]{0:T(128)S(1)} %compare_select_fusion.1, bf16[92,256,64]{1,2,0:T(8,128)(2,1)S(1)} %copy-done), kind=kCustom, calls=%fused_computation.6 | custom fusion | bytes 9044336 | tf_op jit(solution)/shard_map/scatter | solution.py:62
  271.5 3.5 all-to-all-start.2
  275.8 77.5 %all-gather.5.cloned.1.call-done = bf16[16384,64]{0,1:T(8,128)(2,1)} async-done(((bf16[512,64]{0,1:T(8,128)(2,1)}), bf16[16384,64]{0,1:T(8,128)(2,1)}) %all-gather.5.cloned.1.call-update) | async-done | bytes 2097168 | tf_op jit(solution)/shard_map/all_gather | solution.py:50
  355.2 2.5 gather_fusion.2
  357.8 11.7 %fusion.23 = f32[92,256,64]{1,2,0:T(8,128)} fusion(bf16[92,256,256]{2,1,0:T(8,128)(2,1)} %param.13, bf16[92,256,64]{1,2,0:T(8,128)(2,1)} %gather_fusion.2, pred[92]{0:T(512)(128)(4,1)S(1)} %compare_and_fusion), kind=kOutput, calls=%fused_computation.30 | convolution fusion | flops 773259264 | bytes 21102684 | tf_op jit(solution)/shard_map/sij,sjc->sic/dot_general | solution.py:52
  369.4 9.3 %fusion = f32[2,256,64]{1,0,2:T(2,128)S(1)} fusion(f32[92,256,64]{1,2,0:T(8,128)} %fusion.23, f32[92]{0:T(128)S(1)} %fusion.74, s32[92]{0:T(128)S(1)} %get-tuple-element.21), kind=kOutput, calls=%fused_computation.7 | convolution fusion | flops 36176240 | bytes 6161120 | tf_op jit(solution)/shard_map/ks,sic->kic/dot_general | solution.py:65
  378.8 3.7 fusion.37
  383.0 39.7 %all-reduce = (f32[64,64]{0,1:T(8,128)S(1)}, f32[64,64]{0,1:T(8,128)S(1)}) all-reduce(f32[64,64]{0,1:T(8,128)S(1)} %convolution_bitcast_fusion, f32[64,64]{0,1:T(8,128)S(1)} %fusion.76), channel_id=1, replica_groups=mesh['rows'=16,'grp'=2] {'rows','grp'}, use_global_device_ids=true, to_apply=%region_8.13 | all-reduce | flops 8192 | bytes 65536 | tf_op jit(solution)/shard_map/psum | solution.py:75
  422.8 5.8 %cholesky.55 = f32[64,64]{1,0:T(8,128)S(1)} custom-call(f32[64,64]{1,0:T(8,128)S(1)} %fusion.50), custom_call_target="Cholesky" | custom-call | tf_op jit(solution)/shard_map/jit(cholesky)/cholesky | solution.py:79
  430.0 4.9 %custom-call.7 = f32[1,64,64]{1,2,0:T(8,128)S(1)} custom-call(f32[1,64,64]{2,1,0:T(8,128)S(1)} %fusion.48), custom_call_target="InvertDiagBlocksLowerTriangular" | custom-call | tf_op jit(solution)/shard_map/jit(_solve_triangular)/triangular_solve | solution.py:80
  (62 shorter events, 24.0 us)
Async XLA Ops:
  10.3 33.5 %all-to-all-start = ((s32[32,3,1]{1,2,0:T(1,128)}), s32[32,3,1]{1,2,0:T(1,128)S(1)}, u32[]{:S(2)}, u32[]{:S(2)}) async-start(s32[32,3,1]{1,2,0:T(1,128)} %bitcast.3), calls=%async_computation | async-start | bytes 32768 | tf_op jit(solution)/shard_map/all_to_all | solution.py:37
  28.2 3.0 copy-start.1
  43.8 8.1 %copy-start.4 = (s32[92]{0:T(128)S(1)}, s32[92]{0:T(128)}, u32[]{:S(2)}) copy-start(s32[92]{0:T(128)} %param.15) | copy-start | bytes 1108
  43.8 107.2 %all-to-all-start.1 = ((bf16[96,256,64]{1,2,0:T(8,128)(2,1)}), bf16[96,256,64]{1,2,0:T(8,128)(2,1)}, u32[]{:S(2)}, u32[]{:S(2)}) async-start(bf16[96,256,64]{1,2,0:T(8,128)(2,1)} %scatter_fusion), calls=%async_computation.1 | async-start | bytes 6291456 | tf_op jit(solution)/shard_map/all_to_all | solution.py:64
  51.2 74.4 %all-gather.3.cloned.1.call-start = ((), (), s32[]{:S(2)}) async-start(), calls=%async_computation.3 | async-start | bytes 2162688 | tf_op jit(solution)/shard_map/all_gather | solution.py:50
  246.8 0.8 copy-start.2
  256.0 3.0 copy-start
  271.5 107.3 %all-to-all-start.2 = ((bf16[96,256,64]{1,2,0:T(8,128)(2,1)}), bf16[96,256,64]{1,2,0:T(8,128)(2,1)}, u32[]{:S(2)}, u32[]{:S(2)}) async-start(bf16[96,256,64]{1,2,0:T(8,128)(2,1)} %scatter_fusion.1), calls=%async_computation.2 | async-start | bytes 6291456 | tf_op jit(solution)/shard_map/all_to_all | solution.py:64
  275.1 78.3 %all-gather.5.cloned.1.call-start = ((), (), s32[]{:S(2)}) async-start(), calls=%async_computation.4 | async-start | bytes 2162688 | tf_op jit(solution)/shard_map/all_gather | solution.py:50
  378.8 4.0 copy-start.3
Sparse Core Ops, SparseCore 0:
  54.9 70.6 all-gather.2
  279.4 73.9 all-gather.4
